TPU v7x, 32 devices: a whole 2x2x4 slice. The times are simulated.
32 devices in a mesh: groups: 2 (over y), ep: 8 (over z, x), tp: 2 (over core).
Axes of the slice: x: 2, y: 2, z: 4, core: 2. Of those that a mesh axis runs over, the one named last changes fastest.
Arguments:
- hidden: bfloat16 [128, 4096], P(('groups', 'ep', 'tp')), parts along dimension 0, may hold values from -6 to 6
- norm_gain: float32 [4096], replicated, may hold values from 0.5 to 1.5
- rot_left: float32 [64, 64], replicated, may hold values from -0.75 to 0.75
- rot_right: float32 [64, 64], replicated, may hold values from -0.75 to 0.75
- expert_ids: int32 [128, 8], P(('groups', 'ep')), parts along dimension 0, may hold values from 0 to 63, as said below
- gate_weights: float32 [128, 8], P(('groups', 'ep')), parts along dimension 0, may hold values from 0.05 to 1
- w_gate: bfloat16 [128, 4096, 384], P('ep', 'tp'), may hold values from -0.09375 to 0.09375
- w_up: bfloat16 [128, 4096, 384], P('ep', 'tp'), may hold values from -0.09375 to 0.09375
- w_down: bfloat16 [128, 384, 4096], P('ep', None, 'tp'), may hold values from -0.21875 to 0.21875
- unit_scales: float32 [128, 2, 384], P('ep'), may hold values from 0.25 to 1.75
Outputs:
- moe_out: bfloat16 [128, 4096], P(('groups', 'ep', 'tp')), parts along dimension 0
There are 2 independent parts, one for each index of `groups`. A program takes and returns all parts, laid end to end along the dimension named above; an argument that names none is the same for every part. Nothing has to cross between parts.
Inputs may be any that keep to these rules, and one draw needn't show every extreme that they name: `expert_ids`: each row names 8 different experts. In each aligned block of 8 rows (the rows of one index of ep) no expert is named by more than 2 rows, and in every block some experts are named by exactly 2 rows; every expert is named by exactly 2 rows in some block.
All inputs are finite; a program needn't handle non-finite values.
Results may differ from a plain program's by a relative error of at most 0.0082.
Values may be sent and summed in bfloat16 or wider, within the bound.
A program may use at most 128 MiB of HBM per device.

v0:
```python
import functools

import jax
import jax.numpy as jnp
from jax import lax
from jax.experimental import pallas as pl
from jax.experimental.pallas import tpu as pltpu
from jax.sharding import PartitionSpec as P

MESH = pl.DeviceIdType.MESH
HIGH = lax.Precision.HIGHEST
LANES = 128
LAG = 3
UNIT_RING = 10
DOWN_RING = 8


def iota(shape, dim):
    return lax.broadcasted_iota(jnp.int32, shape, dim)


def rotate(hid_ref, gain_ref, left_ref, right_ref, n_tp):
    values = hid_ref[...].astype(jnp.float32)
    rows, width = values.shape
    half = width // n_tp
    order = left_ref.shape[0]
    mean_square = jnp.mean(values * values, axis=1, keepdims=True)
    normed = values * lax.rsqrt(mean_square + 1e-06) * gain_ref[...]
    stacked = jnp.concatenate([normed[:, h * half : (h + 1) * half] for h in range(n_tp)], axis=0)
    groups = half // LANES
    tall = jnp.concatenate(
        [stacked[:, m * LANES : (m + 1) * LANES] for m in range(groups)], axis=0
    )
    per_lane = LANES // order
    tall = jnp.concatenate(
        [tall[:, p * order : (p + 1) * order] for p in range(per_lane)], axis=0
    )
    count = tall.shape[0]
    block = n_tp * rows

    def line_of(index):
        return (
            (index % block) // rows * (half // order)
            + index // block % groups * per_lane
            + index // (block * groups)
        )

    spread = (line_of(iota((count, order), 0)) == iota((count, order), 1)).astype(jnp.float32)
    dims = (((1,), (1,)), ((), ()))
    wide = lax.dot_general(
        jnp.dot(spread, left_ref[...], precision=HIGH, preferred_element_type=jnp.float32),
        spread,
        dims,
        precision=HIGH,
        preferred_element_type=jnp.float32,
    )
    same_row = iota((count, count), 0) % rows == iota((count, count), 1) % rows
    wide = jnp.where(same_row, wide, 0.0)
    turned = lax.dot_general(
        tall, right_ref[...], dims, precision=HIGH, preferred_element_type=jnp.float32
    )
    turned = jnp.dot(wide, turned, precision=HIGH, preferred_element_type=jnp.float32)
    step = count // per_lane
    flat = jnp.concatenate([turned[p * step : (p + 1) * step] for p in range(per_lane)], axis=1)
    return jnp.concatenate([flat[m * block : (m + 1) * block] for m in range(groups)], axis=1)


def routing(ids_ref, weights_ref, experts, capacity):
    ids = ids_ref[...]
    weights = weights_ref[...]
    rows, choices = ids.shape
    weights = weights / jnp.sum(weights, axis=1, keepdims=True)
    weights = weights.astype(jnp.bfloat16).astype(jnp.float32)
    lane = iota((rows, capacity * experts), 1)
    expert = lane % experts
    named = jnp.zeros(lane.shape, jnp.float32)
    value = jnp.zeros(lane.shape, jnp.float32)
    for k in range(choices):
        hit = (ids[:, k : k + 1] == expert).astype(jnp.float32)
        named = named + hit
        value = value + hit * weights[:, k : k + 1]
    row = iota(lane.shape, 0)
    rank = jnp.zeros(lane.shape, jnp.float32)
    for r in range(rows):
        rank = rank + jnp.where(row > r, named[r : r + 1, :], 0.0)
    return jnp.where(rank == (lane // experts).astype(jnp.float32), value, 0.0)


def kernel(
    sizes,
    hid_ref,
    gain_ref,
    left_ref,
    right_ref,
    ids_ref,
    weights_ref,
    scales_ref,
    gate_hbm,
    up_hbm,
    down_hbm,
    out_ref,
    gate_buf,
    up_buf,
    down_buf,
    row_out,
    row_in,
    route_out,
    route_in,
    rows_f32,
    route_t,
    lines,
    part_out,
    part_in,
    values,
    back_out,
    back_in,
    gate_sem,
    up_sem,
    down_sem,
    part_send,
    part_recv,
    plain_sem,
):
    n_ep, n_tp, capacity = sizes
    peers = n_ep * n_tp
    ep = lax.axis_index("ep")
    tp = lax.axis_index("tp")
    me = ep * n_tp + tp
    held = gate_hbm.shape[0]
    unit_ring = gate_buf.shape[0]
    down_ring = down_buf.shape[0]
    rows = hid_ref.shape[0]
    half = row_in.shape[2]
    block = rows * n_tp
    slots = capacity * n_ep
    ff = gate_hbm.shape[2]
    experts = held * n_ep // 2
    total_rows = n_ep * block

    def unit_copies(j, slot):
        return (
            pltpu.make_async_copy(gate_hbm.at[j], gate_buf.at[slot], gate_sem.at[slot]),
            pltpu.make_async_copy(up_hbm.at[j], up_buf.at[slot], up_sem.at[slot]),
        )

    def down_copy(j, slot):
        return pltpu.make_async_copy(down_hbm.at[j], down_buf.at[slot], down_sem.at[slot])

    for j in range(max(unit_ring, down_ring + LAG)):
        if j < unit_ring:
            for copy in unit_copies(j, j):
                copy.start()
        if LAG <= j < down_ring + LAG:
            down_copy(j - LAG, j - LAG).start()

    barrier = pltpu.get_barrier_semaphore()

    def peer_of(offset):
        peer = lax.rem(me + offset, peers)
        return {"ep": peer // n_tp, "tp": lax.rem(peer, n_tp)}, peer

    @pl.loop(1, peers)
    def _(offset):
        where, _peer = peer_of(offset)
        pl.semaphore_signal(barrier, inc=1, device_id=where, device_id_type=MESH)

    route = routing(ids_ref, weights_ref, experts, capacity)
    route_out[...] = route
    route_in[ep] = route
    rotated = rotate(hid_ref, gain_ref, left_ref, right_ref, n_tp).astype(jnp.float32)
    for h in range(n_tp):
        row_out[h] = rotated[h * rows : (h + 1) * rows].astype(jnp.bfloat16)
    row_in[me] = row_out[tp]

    pl.semaphore_wait(barrier, peers - 1)

    @pl.loop(1, n_ep)
    def _(offset):
        pltpu.make_async_remote_copy(
            src_ref=route_out,
            dst_ref=route_in.at[ep],
            send_sem=plain_sem.at[0],
            recv_sem=plain_sem.at[1],
            device_id={"ep": lax.rem(ep + offset, n_ep), "tp": tp},
            device_id_type=MESH,
        ).start()

    @pl.loop(1, peers)
    def _(offset):
        where, peer = peer_of(offset)
        pltpu.make_async_remote_copy(
            src_ref=row_out.at[lax.rem(peer, n_tp)],
            dst_ref=row_in.at[me],
            send_sem=plain_sem.at[2],
            recv_sem=plain_sem.at[3],
            device_id=where,
            device_id_type=MESH,
        ).start()

    def drain(ref, count, sem):
        view = ref.at[pl.ds(0, count)]
        pltpu.make_async_copy(view, view, sem).wait()

    drain(route_in, n_ep - 1, plain_sem.at[1])
    route_t[...] = route_in[...].reshape(total_rows, capacity * experts).T
    first = lax.rem(ep * held, experts)
    owner = (iota((n_ep, total_rows), 1) // block == iota((n_ep, total_rows), 0)).astype(jnp.float32)
    picks = []
    for c in range(capacity):
        line = route_t[pl.ds(c * experts + first, held), :]
        picks.append((line[:, None, :] * owner[None, :, :])[:, None])
    weighted = jnp.concatenate(picks, axis=1).reshape(held * slots, total_rows)
    chosen = jnp.where(weighted > 0.0, 1.0, 0.0).astype(jnp.bfloat16)
    mixing = weighted.T.astype(jnp.bfloat16)

    drain(row_in, peers - 1, plain_sem.at[3])

    @pl.loop(0, n_ep)
    def _(b):
        both = [row_in[b * n_tp + h].astype(jnp.float32) for h in range(n_tp)]
        rows_f32[pl.ds(pl.multiple_of(b * block, block), block), :] = jnp.concatenate(both, axis=0)

    lines[...] = (
        jnp.dot(chosen, rows_f32[...].astype(jnp.bfloat16), preferred_element_type=jnp.float32)
        .astype(jnp.bfloat16)
        .reshape(lines.shape)
    )

    def part_copy(j):
        return pltpu.make_async_remote_copy(
            src_ref=part_out.at[j],
            dst_ref=part_in.at[j],
            send_sem=part_send.at[j],
            recv_sem=part_recv.at[j],
            device_id={"ep": ep, "tp": 1 - tp},
            device_id_type=MESH,
        )

    @pl.loop(0, held + LAG)
    def _(t):
        @pl.when(t < held)
        def _():
            slot = lax.rem(t, unit_ring)
            for copy in unit_copies(t, slot):
                copy.wait()
            line = lines[t]
            part_out[t, :, pl.ds(0, ff)] = jnp.dot(
                line, gate_buf[slot], preferred_element_type=jnp.float32
            )
            part_out[t, :, pl.ds(ff, ff)] = jnp.dot(
                line, up_buf[slot], preferred_element_type=jnp.float32
            )
            part_copy(t).start()

            @pl.when(t + unit_ring < held)
            def _():
                for copy in unit_copies(t + unit_ring, slot):
                    copy.start()

        @pl.when(t >= LAG)
        def _():
            j = t - LAG
            slot = lax.rem(j, down_ring)
            part_copy(j).wait_recv()
            scale = scales_ref[j]
            gate = (part_out[j, :, pl.ds(0, ff)] + part_in[j, :, pl.ds(0, ff)]) * scale[0:1]
            up = (part_out[j, :, pl.ds(ff, ff)] + part_in[j, :, pl.ds(ff, ff)]) * scale[1:2]
            units = (gate / (1.0 + jnp.exp(-gate)) * up).astype(jnp.bfloat16)
            down_copy(j, slot).wait()
            values[pl.ds(pl.multiple_of(j * slots, slots), slots), :] = jnp.dot(
                units, down_buf[slot], preferred_element_type=jnp.float32
            ).astype(jnp.bfloat16)

            @pl.when(j + down_ring < held)
            def _():
                down_copy(j + down_ring, slot).start()

    rows_f32[...] = jnp.dot(mixing, values[...], preferred_element_type=jnp.float32)

    @pl.loop(0, n_ep)
    def _(b):
        both = rows_f32[pl.ds(pl.multiple_of(b * block, block), block), :]
        for h in range(n_tp):
            back_out[b * n_tp + h] = both[h * rows : (h + 1) * rows].astype(jnp.bfloat16)

    back_in[me] = back_out[me]

    @pl.loop(1, peers)
    def _(offset):
        where, peer = peer_of(offset)
        pltpu.make_async_remote_copy(
            src_ref=back_out.at[peer],
            dst_ref=back_in.at[me],
            send_sem=plain_sem.at[4],
            recv_sem=plain_sem.at[5],
            device_id=where,
            device_id_type=MESH,
        ).start()

    @pl.loop(0, held)
    def _(j):
        part_copy(j).wait_send()

    drain(route_in, n_ep - 1, plain_sem.at[0])
    drain(row_in, peers - 1, plain_sem.at[2])
    drain(back_in, peers - 1, plain_sem.at[5])
    for h in range(n_tp):
        def add(e, total):
            return total + back_in[e * n_tp + h].astype(jnp.float32)

        total = lax.fori_loop(0, n_ep, add, jnp.zeros((rows, half), jnp.float32))
        out_ref[:, h * half : (h + 1) * half] = total.astype(jnp.bfloat16)
    drain(back_in, peers - 1, plain_sem.at[4])


def body(
    hidden,
    norm_gain,
    rot_left,
    rot_right,
    expert_ids,
    gate_weights,
    w_gate,
    w_up,
    w_down,
    unit_scales,
):
    n_ep, n_tp = lax.axis_size("ep"), lax.axis_size("tp")
    peers = n_ep * n_tp
    rows, width = hidden.shape
    group_rows, choices = expert_ids.shape
    held, half, ff = w_gate.shape
    experts = held * n_ep // 2
    capacity = 5 * group_rows * choices // (2 * experts)
    slots = capacity * n_ep
    total_rows = n_ep * group_rows
    unit_ring, down_ring = min(UNIT_RING, held), min(DOWN_RING, held)
    vmem = pl.BlockSpec(memory_space=pltpu.VMEM)
    hbm = pl.BlockSpec(memory_space=pl.ANY)
    return pl.pallas_call(
        functools.partial(kernel, (n_ep, n_tp, capacity)),
        out_shape=jax.ShapeDtypeStruct((rows, width), jnp.bfloat16),
        in_specs=[vmem] * 7 + [hbm] * 3,
        out_specs=vmem,
        scratch_shapes=[
            pltpu.VMEM((unit_ring, half, ff), jnp.bfloat16),
            pltpu.VMEM((unit_ring, half, ff), jnp.bfloat16),
            pltpu.VMEM((down_ring, ff, half), jnp.bfloat16),
            pltpu.VMEM((n_tp, rows, half), jnp.bfloat16),
            pltpu.VMEM((peers, rows, half), jnp.bfloat16),
            pltpu.VMEM((group_rows, capacity * experts), jnp.float32),
            pltpu.VMEM((n_ep, group_rows, capacity * experts), jnp.float32),
            pltpu.VMEM((total_rows, half), jnp.float32),
            pltpu.VMEM((capacity * experts, total_rows), jnp.float32),
            pltpu.VMEM((held, slots, half), jnp.bfloat16),
            pltpu.VMEM((held, slots, 2 * ff), jnp.float32),
            pltpu.VMEM((held, slots, 2 * ff), jnp.float32),
            pltpu.VMEM((held * slots, half), jnp.bfloat16),
            pltpu.VMEM((peers, rows, half), jnp.bfloat16),
            pltpu.VMEM((peers, rows, half), jnp.bfloat16),
            pltpu.SemaphoreType.DMA((unit_ring,)),
            pltpu.SemaphoreType.DMA((unit_ring,)),
            pltpu.SemaphoreType.DMA((down_ring,)),
            pltpu.SemaphoreType.DMA((held,)),
            pltpu.SemaphoreType.DMA((held,)),
            pltpu.SemaphoreType.DMA((6,)),
        ],
        compiler_params=pltpu.CompilerParams(
            collective_id=0, has_side_effects=True, vmem_limit_bytes=62 * 1024 * 1024
        ),
    )(
        hidden,
        norm_gain.reshape(1, width),
        rot_left,
        rot_right,
        expert_ids,
        gate_weights,
        unit_scales,
        w_gate,
        w_up,
        w_down,
    )


def solution(mesh):
    placed = (
        P(("groups", "ep", "tp"), None),
        P(),
        P(),
        P(),
        P(("groups", "ep"), None),
        P(("groups", "ep"), None),
        P("ep", "tp", None),
        P("ep", "tp", None),
        P("ep", None, "tp"),
        P("ep", None, None),
    )
    return jax.shard_map(
        body, mesh=mesh, in_specs=placed, out_specs=P(("groups", "ep", "tp"), None), check_vma=False
    )
```

profile of v0, /device:TPU:0, one launch (start us, length us, event | category | flops | bytes accessed | tf_op | source)
XLA Modules:
  0.0 37.9 jit_solution(13674756736429877058)
XLA Ops:
  0.0 36.5 %shard_map.100 = bf16[4,4096]{1,0:T(4,128)(2,1)} custom-call(bf16[4,4096]{1,0:T(4,128)(2,1)} %hid_ref.1, f32[1,4096]{1,0:T(1,128)} %bitcast.1, f32[64,64]{1,0:T(8,128)} %left_ref.1, f32[64,64]{1,0:T(8,128)} %right_ref.1, s32[8,8]{1,0:T(8,128)} %ids_ref.1, f32[8,8]{1,0:T(8,128)} %weights_ref.1, f32[16,2,384]{2,1,0:T(2,128)} %scales_ref.1, ...), custom_call_target="tpu_custom_call" | custom-call | tf_op jit(solution)/shard_map/pallas_call | solution.py:340
  36.5 1.4 %copy.12 = bf16[4,4096]{1,0:T(4,128)(2,1)} copy(bf16[4,4096]{1,0:T(4,128)(2,1)} %shard_map.100) | data formatting | bytes 65536
where the time goes:
time: 38.1 us; the launch traced here: 37.9 us
  Pallas kernels  36.5 us (96%)
  local copies, waits for them, and re-layouts  1.39 us (4%)
    pallas_call x1, Pallas kernels, body(): pl.pallas_call(functools.partial(kernel, (n_ep, n_tp, capacity)), out_sha...  36.5 us
    unnamed x1, local copies, waits for them, and re-layouts  1.39 us

commit v1 on v0

v1 whole, which is shorter than its diff:
```python
import functools

import jax
import jax.numpy as jnp
from jax import lax
from jax.experimental import pallas as pl
from jax.experimental.pallas import tpu as pltpu
from jax.sharding import PartitionSpec as P

MESH = pl.DeviceIdType.MESH
HIGH = lax.Precision.HIGHEST
LANES = 128
SUBLANES = 8
PAIR = 2
LAG = 2
SPLIT = 2
UNIT_RING = 14
DOWN_RING = 9
EARLY = 2
GROUP = 4
CHUNKS = 4
UNROLL = 32


def iota(shape, dim):
    return lax.broadcasted_iota(jnp.int32, shape, dim)


def rotate(hid_ref, gain_ref, left_ref, right_ref, n_tp):
    values = hid_ref[...].astype(jnp.float32)
    rows, width = values.shape
    half = width // n_tp
    order = left_ref.shape[0]
    mean_square = jnp.mean(values * values, axis=1, keepdims=True)
    normed = values * lax.rsqrt(mean_square + 1e-06) * gain_ref[...]
    stacked = jnp.concatenate([normed[:, h * half : (h + 1) * half] for h in range(n_tp)], axis=0)
    groups = half // LANES
    tall = jnp.concatenate(
        [stacked[:, m * LANES : (m + 1) * LANES] for m in range(groups)], axis=0
    )
    per_lane = LANES // order
    tall = jnp.concatenate(
        [tall[:, p * order : (p + 1) * order] for p in range(per_lane)], axis=0
    )
    count = tall.shape[0]
    block = n_tp * rows

    def line_of(index):
        return (
            (index % block) // rows * (half // order)
            + index // block % groups * per_lane
            + index // (block * groups)
        )

    spread = (line_of(iota((count, order), 0)) == iota((count, order), 1)).astype(jnp.float32)
    dims = (((1,), (1,)), ((), ()))
    wide = lax.dot_general(
        jnp.dot(spread, left_ref[...], precision=HIGH, preferred_element_type=jnp.float32),
        spread,
        dims,
        precision=HIGH,
        preferred_element_type=jnp.float32,
    )
    same_row = iota((count, count), 0) % rows == iota((count, count), 1) % rows
    wide = jnp.where(same_row, wide, 0.0)
    turned = lax.dot_general(
        tall, right_ref[...], dims, precision=HIGH, preferred_element_type=jnp.float32
    )
    turned = jnp.dot(wide, turned, precision=HIGH, preferred_element_type=jnp.float32)
    step = count // per_lane
    flat = jnp.concatenate([turned[p * step : (p + 1) * step] for p in range(per_lane)], axis=1)
    return jnp.concatenate([flat[m * block : (m + 1) * block] for m in range(groups)], axis=1)


def routing(ids_ref, weights_ref, experts, capacity):
    ids = ids_ref[...]
    weights = weights_ref[...]
    rows, choices = ids.shape
    weights = weights / jnp.sum(weights, axis=1, keepdims=True)
    weights = weights.astype(jnp.bfloat16).astype(jnp.float32)
    lane = iota((rows, capacity * experts), 1)
    expert = lane % experts
    named = jnp.zeros(lane.shape, jnp.float32)
    value = jnp.zeros(lane.shape, jnp.float32)
    for k in range(choices):
        hit = (ids[:, k : k + 1] == expert).astype(jnp.float32)
        named = named + hit
        value = value + hit * weights[:, k : k + 1]
    row = iota(lane.shape, 0)
    rank = jnp.zeros(lane.shape, jnp.float32)
    for r in range(rows):
        rank = rank + jnp.where(row > r, named[r : r + 1, :], 0.0)
    return jnp.where(rank == (lane // experts).astype(jnp.float32), value, 0.0)


def kernel(
    sizes,
    hid_hbm,
    gain_hbm,
    left_hbm,
    right_hbm,
    ids_hbm,
    weights_hbm,
    scales_hbm,
    gate_hbm,
    up_hbm,
    down_hbm,
    out_ref,
    hid_ref,
    gain_ref,
    left_ref,
    right_ref,
    ids_ref,
    weights_ref,
    scales_ref,
    unit_buf,
    down_buf,
    row_out,
    row_in,
    route_out,
    route_in,
    route_t,
    lines,
    part_out,
    part_in,
    units,
    mixing,
    values,
    back_out,
    back_in,
    unit_sem,
    down_sem,
    part_recv,
    row_recv,
    back_recv,
    plain_sem,
):
    n_ep, n_tp, capacity = sizes
    peers = n_ep * n_tp
    ep = lax.axis_index("ep")
    tp = lax.axis_index("tp")
    me = ep * n_tp + tp
    held, half, ff = gate_hbm.shape
    unit_ring, pair, deep, _ = unit_buf.shape
    down_ring, group, _, wide = down_buf.shape
    rows = hid_ref.shape[0]
    fold = SUBLANES // rows
    block = rows * n_tp
    slots = capacity * n_ep
    experts = held * n_ep // 2
    padded = peers * SUBLANES
    split = half // deep
    thin = deep // fold
    chunks = half // wide
    parts = held // group
    items = chunks * parts
    steps = held // pair
    pieces = split * steps
    lag = min(LAG, steps)
    slim = wide // fold

    barrier = pltpu.get_barrier_semaphore()

    def start_unit(i, slot):
        k, s = i // steps, lax.rem(i, steps)
        for source, at in ((gate_hbm, 0), (up_hbm, ff)):
            pltpu.make_async_copy(
                source.at[pl.ds(s * pair, pair), pl.ds(pl.multiple_of(k * deep, deep), deep)],
                unit_buf.at[slot, :, :, pl.ds(at, ff)],
                unit_sem.at[slot],
            ).start()

    def start_down(i, slot):
        c, q = i // parts, lax.rem(i, parts)
        pltpu.make_async_copy(
            down_hbm.at[pl.ds(q * group, group), :, pl.ds(pl.multiple_of(c * wide, wide), wide)],
            down_buf.at[slot],
            down_sem.at[slot],
        ).start()

    def start_downs():
        for i in range(down_ring):
            start_down(jnp.int32(i), i)

    def landed(ref, sem):
        pltpu.make_async_copy(ref, ref, sem).wait()

    def drain(ref, count, sem):
        landed(ref.at[pl.ds(0, count)], sem)

    def each(first, count, act):
        if count <= UNROLL:
            for offset in range(first, count):
                act(offset)
        else:
            pl.loop(first, count)(act)

    def each_peer(act):
        def visit(offset):
            peer = lax.rem(me + offset, peers)
            act({"ep": peer // n_tp, "tp": lax.rem(peer, n_tp)}, peer)

        each(1, peers, visit)

    small = [
        pltpu.make_async_copy(source, target, plain_sem.at[4])
        for source, target in (
            (hid_hbm, hid_ref),
            (gain_hbm, gain_ref),
            (left_hbm, left_ref),
            (right_hbm, right_ref),
            (ids_hbm, ids_ref),
            (weights_hbm, weights_ref),
            (scales_hbm, scales_ref),
        )
    ]
    for copy in small:
        copy.start()
    each_peer(
        lambda where, peer: pl.semaphore_signal(barrier, inc=1, device_id=where, device_id_type=MESH)
    )
    early = min(EARLY, unit_ring)
    for i in range(early):
        start_unit(jnp.int32(i), i)
    for copy in small:
        copy.wait()

    route = routing(ids_ref, weights_ref, experts, capacity)
    route_out[...] = route
    route_in[ep] = route
    rotated = rotate(hid_ref, gain_ref, left_ref, right_ref, n_tp).astype(jnp.float32)
    for k in range(split):
        for h in range(n_tp):
            line = rotated[h * rows : (h + 1) * rows, k * deep : (k + 1) * deep]
            line = jnp.concatenate([line[:, f * thin : (f + 1) * thin] for f in range(fold)], axis=0)
            row_out[k, h] = line.astype(jnp.bfloat16)
        row_in[k, me] = row_out[k, tp]

    pl.semaphore_wait(barrier, peers - 1)

    def send_route(offset):
        pltpu.make_async_remote_copy(
            src_ref=route_out,
            dst_ref=route_in.at[ep],
            send_sem=plain_sem.at[0],
            recv_sem=plain_sem.at[1],
            device_id={"ep": lax.rem(ep + offset, n_ep), "tp": tp},
            device_id_type=MESH,
        ).start()

    def send_row(k):
        def act(where, peer):
            pltpu.make_async_remote_copy(
                src_ref=row_out.at[k, lax.rem(peer, n_tp)],
                dst_ref=row_in.at[k, me],
                send_sem=plain_sem.at[2],
                recv_sem=row_recv.at[k],
                device_id=where,
                device_id_type=MESH,
            ).start()

        return act

    each(1, n_ep, send_route)
    for k in range(split):
        each_peer(send_row(k))

    for i in range(early, unit_ring):
        start_unit(jnp.int32(i), i)
    if pieces <= unit_ring:
        start_downs()

    drain(route_in, n_ep - 1, plain_sem.at[1])
    spread = []
    for b in range(n_ep):
        for h in range(n_tp):
            spread.append(route_in[b, h * rows : (h + 1) * rows, :])
            spread.append(jnp.zeros((SUBLANES - rows, capacity * experts), jnp.float32))
    route_t[...] = jnp.concatenate(spread, axis=0).T
    first = lax.rem(ep * held, experts)
    owner = (
        iota((n_ep, padded), 1) // (n_tp * SUBLANES) == iota((n_ep, padded), 0)
    ).astype(jnp.float32)
    picks = []
    for c in range(capacity):
        line = route_t[pl.ds(c * experts + first, held), :]
        picks.append((line[:, None, :] * owner[None, :, :])[:, None])
    weighted = jnp.concatenate(picks, axis=1).reshape(held * slots, padded)
    shifted = [weighted] + [pltpu.roll(weighted, f * rows, 1) for f in range(1, fold)]
    chosen = jnp.concatenate(shifted, axis=0)
    chosen = jnp.where(chosen > 0.0, 1.0, 0.0).astype(jnp.bfloat16)
    for f in range(fold):
        mixing[:, f * held * slots : (f + 1) * held * slots] = shifted[f].T.astype(jnp.bfloat16)

    def select(k):
        picked = jnp.dot(
            chosen, row_in[k].reshape(padded, thin), preferred_element_type=jnp.float32
        ).astype(jnp.bfloat16)
        for f in range(fold):
            lines[k, :, :, f * thin : (f + 1) * thin] = picked[
                f * held * slots : (f + 1) * held * slots
            ].reshape(held, slots, thin)

    def part_copy(s):
        return pltpu.make_async_remote_copy(
            src_ref=part_out.at[pl.ds(s * pair, pair)],
            dst_ref=part_in.at[pl.ds(s * pair, pair)],
            send_sem=plain_sem.at[0],
            recv_sem=part_recv.at[s],
            device_id={"ep": ep, "tp": 1 - tp},
            device_id_type=MESH,
        )

    def finish(s):
        for p in range(pair):
            j = s * pair + p
            scale = scales_ref[j]
            gate = (part_out[j, :, pl.ds(0, ff)] + part_in[j, :, pl.ds(0, ff)]) * scale[0:1]
            up = (part_out[j, :, pl.ds(ff, ff)] + part_in[j, :, pl.ds(ff, ff)]) * scale[1:2]
            units[j] = (gate / (1.0 + jnp.exp(-gate)) * up).astype(jnp.bfloat16)

    def project(k, s, slot):
        for p in range(pair):
            j = s * pair + p
            total = jnp.dot(lines[k, j], unit_buf[slot, p], preferred_element_type=jnp.float32)
            if k > 0:
                total = total + part_out[j]
            part_out[j] = total

    def step(k, s, both):
        i = k * steps + s
        slot = lax.rem(i, unit_ring)
        landed(unit_buf.at[slot], unit_sem.at[slot])
        if both:
            part_copy(s - lag).wait_recv()
            finish(s - lag)
        project(k, s, slot)
        if k == split - 1:
            part_copy(s).start()
        if pieces > unit_ring:

            @pl.when(i + unit_ring < pieces)
            def _():
                start_unit(i + unit_ring, slot)

            @pl.when(i + unit_ring == pieces - 1)
            def _():
                start_downs()

    drain(route_in, n_ep - 1, plain_sem.at[0])
    for k in range(split):
        drain(row_in.at[k], peers - 1, row_recv.at[k])
        select(k)
        if k < split - 1:

            @pl.loop(0, steps)
            def _(s):
                step(k, s, False)

    for s in range(lag):
        step(split - 1, jnp.int32(s), False)

    @pl.loop(lag, steps)
    def _(s):
        step(split - 1, s, True)

    def down_wait(c, q):
        slot = lax.rem(c * parts + q, down_ring)
        landed(down_buf.at[slot], down_sem.at[slot])

    def down_part(c, q):
        slot = lax.rem(c * parts + q, down_ring)
        for p in range(group):
            j = q * group + p
            value = jnp.dot(units[j], down_buf[slot, p], preferred_element_type=jnp.float32)
            for f in range(fold):
                at = f * held * slots + j * slots
                values[at : at + slots, :] = value[:, f * slim : (f + 1) * slim].astype(jnp.bfloat16)

    def down_next(c, q):
        i = c * parts + q

        @pl.when(i + down_ring < items)
        def _():
            start_down(i + down_ring, lax.rem(i, down_ring))

    def give(c):
        mixed = jnp.dot(mixing[...], values[...], preferred_element_type=jnp.float32)
        back_out[c] = mixed.astype(jnp.bfloat16).reshape(peers, SUBLANES, slim)
        back_in[c, me] = back_out[c, me]

        def act(where, peer):
            pltpu.make_async_remote_copy(
                src_ref=back_out.at[c, peer],
                dst_ref=back_in.at[c, me],
                send_sem=plain_sem.at[3],
                recv_sem=back_recv.at[c],
                device_id=where,
                device_id_type=MESH,
            ).start()

        each_peer(act)

    ready = (steps - lag) * pair // group
    zero = jnp.int32(0)
    for q in range(ready):
        down_wait(zero, q)
        down_part(zero, q)
        down_next(zero, q)
    for s in range(steps - lag, steps):
        part_copy(jnp.int32(s)).wait_recv()
        finish(jnp.int32(s))
    for q in range(ready, parts):
        down_wait(zero, q)
        down_part(zero, q)
        down_next(zero, q)
    give(zero)

    @pl.loop(1, chunks)
    def _(c):
        for q in range(parts):
            down_wait(c, q)
            down_part(c, q)
            down_next(c, q)
        give(c)

    for c in range(chunks):
        drain(back_in.at[c], peers - 1, back_recv.at[c])
        for h in range(n_tp):
            total = back_in[c, h].astype(jnp.float32)
            for e in range(1, n_ep):
                total = total + back_in[c, e * n_tp + h].astype(jnp.float32)
            for f in range(fold):
                at = h * half + c * wide + f * slim
                out_ref[:, at : at + slim] = total[f * rows : (f + 1) * rows].astype(jnp.bfloat16)
    landed(part_out, plain_sem.at[0])
    for k in range(split):
        drain(row_in.at[k], peers - 1, plain_sem.at[2])
    for c in range(chunks):
        drain(back_in.at[c], peers - 1, plain_sem.at[3])


def body(
    hidden,
    norm_gain,
    rot_left,
    rot_right,
    expert_ids,
    gate_weights,
    w_gate,
    w_up,
    w_down,
    unit_scales,
):
    n_ep, n_tp = lax.axis_size("ep"), lax.axis_size("tp")
    peers = n_ep * n_tp
    rows, width = hidden.shape
    group_rows, choices = expert_ids.shape
    held, half, ff = w_gate.shape
    experts = held * n_ep // 2
    capacity = 5 * group_rows * choices // (2 * experts)
    slots = capacity * n_ep
    unit_pair = PAIR if held % PAIR == 0 else 1
    steps = held // unit_pair
    unit_ring = min(UNIT_RING, SPLIT * steps)
    deep = half // SPLIT
    group = min(GROUP, held)
    wide = half // CHUNKS
    down_ring = min(DOWN_RING, held // group * CHUNKS)
    fold = SUBLANES // rows
    padded = peers * SUBLANES
    small = (
        hidden,
        norm_gain.reshape(1, width),
        rot_left,
        rot_right,
        expert_ids,
        gate_weights,
        unit_scales,
    )
    return pl.pallas_call(
        functools.partial(kernel, (n_ep, n_tp, capacity)),
        out_shape=pltpu.VMEM((rows, width), jnp.bfloat16),
        in_specs=[pl.BlockSpec(memory_space=pltpu.HBM)] * 10,
        out_specs=pl.BlockSpec(memory_space=pltpu.VMEM),
        scratch_shapes=[pltpu.VMEM(x.shape, x.dtype) for x in small]
        + [
            pltpu.VMEM((unit_ring, unit_pair, deep, 2 * ff), jnp.bfloat16),
            pltpu.VMEM((down_ring, group, ff, wide), jnp.bfloat16),
            pltpu.VMEM((SPLIT, n_tp, SUBLANES, deep // fold), jnp.bfloat16),
            pltpu.VMEM((SPLIT, peers, SUBLANES, deep // fold), jnp.bfloat16),
            pltpu.VMEM((group_rows, capacity * experts), jnp.float32),
            pltpu.VMEM((n_ep, group_rows, capacity * experts), jnp.float32),
            pltpu.VMEM((capacity * experts, padded), jnp.float32),
            pltpu.VMEM((SPLIT, held, slots, deep), jnp.bfloat16),
            pltpu.VMEM((held, slots, 2 * ff), jnp.float32),
            pltpu.VMEM((held, slots, 2 * ff), jnp.float32),
            pltpu.VMEM((held, slots, ff), jnp.bfloat16),
            pltpu.VMEM((padded, fold * held * slots), jnp.bfloat16),
            pltpu.VMEM((fold * held * slots, wide // fold), jnp.bfloat16),
            pltpu.VMEM((CHUNKS, peers, SUBLANES, wide // fold), jnp.bfloat16),
            pltpu.VMEM((CHUNKS, peers, SUBLANES, wide // fold), jnp.bfloat16),
            pltpu.SemaphoreType.DMA((unit_ring,)),
            pltpu.SemaphoreType.DMA((down_ring,)),
            pltpu.SemaphoreType.DMA((steps,)),
            pltpu.SemaphoreType.DMA((SPLIT,)),
            pltpu.SemaphoreType.DMA((CHUNKS,)),
            pltpu.SemaphoreType.DMA((5,)),
        ],
        compiler_params=pltpu.CompilerParams(
            collective_id=0, has_side_effects=True, vmem_limit_bytes=63 * 1024 * 1024
        ),
    )(*small, w_gate, w_up, w_down)


def solution(mesh):
    placed = (
        P(("groups", "ep", "tp"), None),
        P(),
        P(),
        P(),
        P(("groups", "ep"), None),
        P(("groups", "ep"), None),
        P("ep", "tp", None),
        P("ep", "tp", None),
        P("ep", None, "tp"),
        P("ep", None, None),
    )
    return jax.shard_map(
        body, mesh=mesh, in_specs=placed, out_specs=P(("groups", "ep", "tp"), None), check_vma=False
    )
```

time: 38.1 us -> 35.2 us (0.924)
  Pallas kernels: 36.5 us -> 34.4 us
  local copies, waits for them, and re-layouts: 1.39 us -> 0.62 us
    pallas_call x1, Pallas kernels: 36.5 us -> 34.4 us  [body(): pl.pallas_call(functools.partial(kernel, (n_ep, n_tp, capacity)), out_sha...]
    unnamed x1, local copies, waits for them, and re-layouts: 1.39 us -> 0.62 us
where the time goes in v1:
time: 35.2 us; the launch traced here: 35 us
  Pallas kernels  34.4 us (98%)
  local copies, waits for them, and re-layouts  0.62 us (2%)
    pallas_call x1, Pallas kernels, body(): pl.pallas_call(functools.partial(kernel, (n_ep, n_tp, capacity)), out_sha...  34.4 us

profile of v1, /device:TPU:0, one launch (start us, length us, event | category | flops | bytes accessed | tf_op | source)
XLA Modules:
  0.0 35.0 jit_solution(11694587991048071041)
XLA Ops:
  0.0 34.4 %shard_map.100 = bf16[4,4096]{1,0:T(4,128)(2,1)S(1)} custom-call(bf16[4,4096]{1,0:T(4,128)(2,1)} %hid_hbm.1, f32[1,4096]{1,0:T(1,128)} %bitcast.1, f32[64,64]{1,0:T(8,128)} %left_hbm.1, f32[64,64]{1,0:T(8,128)} %right_hbm.1, s32[8,8]{1,0:T(8,128)} %ids_hbm.1, f32[8,8]{1,0:T(8,128)} %weights_hbm.1, f32[16,2,384]{2,1,0:T(2,128)} %scales_hbm.1, ...), custom_call_target="tpu_custom_call" | custom-call | tf_op jit(solution)/shard_map/pallas_call | solution.py:481
  34.4 0.6 %copy.12 = bf16[4,4096]{1,0:T(4,128)(2,1)} copy(bf16[4,4096]{1,0:T(4,128)(2,1)S(1)} %shard_map.100) | data formatting | bytes 65536

commit v2 on v1

v2 whole, which is shorter than its diff:
```python
import functools

import jax
import jax.numpy as jnp
from jax import lax
from jax.experimental import pallas as pl
from jax.experimental.pallas import tpu as pltpu
from jax.sharding import PartitionSpec as P

MESH = pl.DeviceIdType.MESH
HIGH = lax.Precision.HIGHEST
LANES = 128
SUBLANES = 8
PASSES = (4, 4, 2)
LAG = 2
MORE = 2
SPAN = 5
UNIT_RING = 14
DOWN_RING = 9
EARLY = 3
WIDTHS = ((1, 8), (2, 4), (2, 4), (2, 4), (1, 4))
UNROLL = 32


def iota(shape, dim):
    return lax.broadcasted_iota(jnp.int32, shape, dim)


def halves(value):
    high = value.astype(jnp.bfloat16)
    return high, (value - high.astype(jnp.float32)).astype(jnp.bfloat16)


def rotate(hid_ref, gain_ref, left_ref, right_ref, n_tp):
    values = hid_ref[...].astype(jnp.float32)
    rows, width = values.shape
    half = width // n_tp
    order = left_ref.shape[0]
    groups = half // LANES
    per_lane = LANES // order
    block = n_tp * rows
    count = block * groups * per_lane

    def line_of(index):
        return (
            (index % block) // rows * (half // order)
            + index // block % groups * per_lane
            + index // (block * groups)
        )

    across = (((1,), (1,)), ((), ()))
    spread = (line_of(iota((count, order), 0)) == iota((count, order), 1)).astype(jnp.bfloat16)
    same_row = iota((count, count), 0) % rows == iota((count, count), 1) % rows
    wide = []
    for part in halves(left_ref[...]):
        tall = jnp.dot(spread, part, preferred_element_type=jnp.float32).astype(jnp.bfloat16)
        full = lax.dot_general(tall, spread, across, preferred_element_type=jnp.float32)
        wide.append(jnp.where(same_row, full, 0.0).astype(jnp.bfloat16))

    mean_square = jnp.mean(values * values, axis=1, keepdims=True)
    normed = values * lax.rsqrt(mean_square + 1e-06) * gain_ref[...]
    stacked = jnp.concatenate([normed[:, h * half : (h + 1) * half] for h in range(n_tp)], axis=0)
    tall = jnp.concatenate(
        [stacked[:, m * LANES : (m + 1) * LANES] for m in range(groups)], axis=0
    )
    tall = jnp.concatenate(
        [tall[:, p * order : (p + 1) * order] for p in range(per_lane)], axis=0
    )

    high, low = halves(tall)
    right_high, right_low = halves(right_ref[...])
    turned = (
        lax.dot_general(high, right_high, across, preferred_element_type=jnp.float32)
        + lax.dot_general(high, right_low, across, preferred_element_type=jnp.float32)
        + lax.dot_general(low, right_high, across, preferred_element_type=jnp.float32)
    )
    high, low = halves(turned)
    turned = (
        jnp.dot(wide[0], high, preferred_element_type=jnp.float32)
        + jnp.dot(wide[0], low, preferred_element_type=jnp.float32)
        + jnp.dot(wide[1], high, preferred_element_type=jnp.float32)
    )
    step = count // per_lane
    flat = jnp.concatenate([turned[p * step : (p + 1) * step] for p in range(per_lane)], axis=1)
    return jnp.concatenate([flat[m * block : (m + 1) * block] for m in range(groups)], axis=1)


def routing(ids_ref, weights_ref, experts, capacity):
    ids = ids_ref[...]
    weights = weights_ref[...]
    rows, choices = ids.shape
    weights = weights / jnp.sum(weights, axis=1, keepdims=True)
    weights = weights.astype(jnp.bfloat16).astype(jnp.float32)
    lane = iota((rows, capacity * experts), 1)
    expert = lane % experts
    named = jnp.zeros(lane.shape, jnp.float32)
    value = jnp.zeros(lane.shape, jnp.float32)
    for k in range(choices):
        hit = (ids[:, k : k + 1] == expert).astype(jnp.float32)
        named = named + hit
        value = value + hit * weights[:, k : k + 1]
    row = iota(lane.shape, 0)
    rank = jnp.zeros(lane.shape, jnp.float32)
    for r in range(rows):
        rank = rank + jnp.where(row > r, named[r : r + 1, :], 0.0)
    return jnp.where(rank == (lane // experts).astype(jnp.float32), value, 0.0)


def passes_of(held, half):
    plan, pieces, begin = [], [], 0
    for share in PASSES:
        deep, count = half // share, share if held % share == 0 else 1
        plan.append((begin, deep, count))
        pieces += [(begin, deep, count, s) for s in range(held // count)]
        begin += deep
    return plan, pieces


def chunks_of(held, half):
    chunks, items, begin = [], [], 0
    unit = half // sum(share for share, _ in WIDTHS)
    for share, count in WIDTHS:
        count = count if held % count == 0 else 1
        chunks.append((begin, share * unit, count))
        items += [(begin, share * unit, count, q) for q in range(held // count)]
        begin += share * unit
    return chunks, items


def kernel(
    sizes,
    hid_hbm,
    gain_hbm,
    left_hbm,
    right_hbm,
    ids_hbm,
    weights_hbm,
    scales_hbm,
    gate_hbm,
    up_hbm,
    down_hbm,
    out_ref,
    hid_ref,
    gain_ref,
    left_ref,
    right_ref,
    ids_ref,
    weights_ref,
    scales_ref,
    unit_buf,
    down_buf,
    row_out,
    row_in,
    route_out,
    route_in,
    route_t,
    lines,
    part_out,
    part_in,
    units,
    mixing,
    values,
    back_out,
    back_in,
    unit_sem,
    down_sem,
    part_recv,
    row_recv,
    back_recv,
    plain_sem,
):
    n_ep, n_tp, capacity = sizes
    peers = n_ep * n_tp
    ep = lax.axis_index("ep")
    tp = lax.axis_index("tp")
    me = ep * n_tp + tp
    held, half, ff = gate_hbm.shape
    unit_ring = unit_buf.shape[0]
    down_ring = down_buf.shape[0]
    rows = hid_ref.shape[0]
    fold = SUBLANES // rows
    block = rows * n_tp
    slots = capacity * n_ep
    experts = held * n_ep // 2
    padded = peers * SUBLANES
    chunks, items = chunks_of(held, half)
    plan, pieces = passes_of(held, half)
    pair = plan[-1][2]
    pairs = held // pair
    more = MORE if pairs % MORE == 0 else 1
    lag = min(LAG, pairs // more)
    again = len(pieces) - unit_ring

    barrier = pltpu.get_barrier_semaphore()

    def start_unit(i):
        begin, deep, count, s = pieces[i]
        slot = i % unit_ring
        for p in range(count):
            for source, at in ((gate_hbm, 0), (up_hbm, ff)):
                pltpu.make_async_copy(
                    source.at[s * count + p, pl.ds(begin, deep)],
                    unit_buf.at[slot, pl.ds(p * deep, deep), pl.ds(at, ff)],
                    unit_sem.at[slot],
                ).start()

    def start_down(i):
        begin, wide, count, q = items[i]
        slot = i % down_ring
        for p in range(count):
            pltpu.make_async_copy(
                down_hbm.at[q * count + p, :, pl.ds(begin, wide)],
                down_buf.at[slot, :, pl.ds(p * wide, wide)],
                down_sem.at[slot],
            ).start()

    ahead = -(-down_ring // min(pairs, SPAN))
    since = pairs - -(-down_ring // ahead)

    def start_downs(s):
        for i in range((s - since) * ahead, min((s - since + 1) * ahead, down_ring)):
            if i >= 0:
                start_down(i)

    def landed(ref, sem):
        pltpu.make_async_copy(ref, ref, sem).wait()

    def drain(ref, count, sem):
        landed(ref.at[pl.ds(0, count)], sem)

    def each(first, count, act):
        if count <= UNROLL:
            for offset in range(first, count):
                act(offset)
        else:
            pl.loop(first, count)(act)

    upper = ep >= n_ep // 2
    own = jnp.where(upper, ep, n_ep - 1 - ep)

    def each_ep(act):
        def visit(i):
            i = i + jnp.where(i >= own, 1, 0)
            act(jnp.where(upper, i, n_ep - 1 - i))

        each(0, n_ep - 1, visit)

    def each_peer(act):
        def visit(to):
            for h in range(n_tp):
                act({"ep": to, "tp": h}, to * n_tp + h, h)

        each_ep(visit)
        for h in range(1, n_tp):
            beside = lax.rem(tp + h, n_tp)
            act({"ep": ep, "tp": beside}, ep * n_tp + beside, beside)

    small = [
        pltpu.make_async_copy(source, target, plain_sem.at[4])
        for source, target in (
            (hid_hbm, hid_ref),
            (gain_hbm, gain_ref),
            (left_hbm, left_ref),
            (right_hbm, right_ref),
            (ids_hbm, ids_ref),
            (weights_hbm, weights_ref),
            (scales_hbm, scales_ref),
        )
    ]
    for copy in small:
        copy.start()
    each_peer(
        lambda where, peer, h: pl.semaphore_signal(
            barrier, inc=1, device_id=where, device_id_type=MESH
        )
    )
    early = min(EARLY, unit_ring)
    for i in range(early):
        start_unit(i)
    for copy in small:
        copy.wait()

    route = routing(ids_ref, weights_ref, experts, capacity)
    route_out[...] = route.astype(jnp.bfloat16)
    route_in[ep] = route_out[...]
    rotated = rotate(hid_ref, gain_ref, left_ref, right_ref, n_tp).astype(jnp.float32)
    for begin, deep, _ in plan:
        thin = deep // fold
        for h in range(n_tp):
            line = rotated[h * rows : (h + 1) * rows, begin : begin + deep]
            line = jnp.concatenate([line[:, f * thin : (f + 1) * thin] for f in range(fold)], axis=0)
            row_out[h, :, begin // fold : begin // fold + thin] = line.astype(jnp.bfloat16)
    row_in[me] = row_out[tp]

    pl.semaphore_wait(barrier, peers - 1)

    def send_route(to):
        pltpu.make_async_remote_copy(
            src_ref=route_out,
            dst_ref=route_in.at[ep],
            send_sem=plain_sem.at[0],
            recv_sem=plain_sem.at[1],
            device_id={"ep": to, "tp": tp},
            device_id_type=MESH,
        ).start()

    def part_of(k):
        return pl.ds(plan[k][0] // fold, plan[k][1] // fold)

    def send_row(k):
        def act(where, peer, h):
            pltpu.make_async_remote_copy(
                src_ref=row_out.at[h, :, part_of(k)],
                dst_ref=row_in.at[me, :, part_of(k)],
                send_sem=plain_sem.at[2],
                recv_sem=row_recv.at[k],
                device_id=where,
                device_id_type=MESH,
            ).start()

        return act

    each_ep(send_route)
    for k in range(len(plan)):
        each_peer(send_row(k))

    for i in range(early, unit_ring):
        start_unit(i)

    drain(route_in, n_ep - 1, plain_sem.at[1])
    spread = []
    for b in range(n_ep):
        for h in range(n_tp):
            spread.append(route_in[b].astype(jnp.float32)[h * rows : (h + 1) * rows, :])
            spread.append(jnp.zeros((SUBLANES - rows, capacity * experts), jnp.float32))
    route_t[...] = jnp.concatenate(spread, axis=0).T
    first = lax.rem(ep * held, experts)
    owner = (
        iota((n_ep, padded), 1) // (n_tp * SUBLANES) == iota((n_ep, padded), 0)
    ).astype(jnp.float32)
    picks = []
    for c in range(capacity):
        line = route_t[pl.ds(c * experts + first, held), :]
        picks.append((line[:, None, :] * owner[None, :, :])[:, None])
    weighted = jnp.concatenate(picks, axis=1).reshape(held * slots, padded)
    shifted = [weighted] + [pltpu.roll(weighted, f * rows, 1) for f in range(1, fold)]
    chosen = jnp.concatenate(shifted, axis=0)
    chosen = jnp.where(chosen > 0.0, 1.0, 0.0).astype(jnp.bfloat16)
    for f in range(fold):
        mixing[f] = shifted[f].T.astype(jnp.bfloat16)

    def select(k):
        begin, deep, _ = plan[k]
        thin = deep // fold
        picked = jnp.dot(
            chosen, row_in[:, :, part_of(k)].reshape(padded, thin), preferred_element_type=jnp.float32
        ).astype(jnp.bfloat16)
        for f in range(fold):
            lines[:, :, begin + f * thin : begin + (f + 1) * thin] = picked[
                f * held * slots : (f + 1) * held * slots
            ].reshape(held, slots, thin)

    def part_copy(t):
        span = pl.ds(t * more * pair, more * pair)
        return pltpu.make_async_remote_copy(
            src_ref=part_out.at[span],
            dst_ref=part_in.at[span],
            send_sem=plain_sem.at[0],
            recv_sem=part_recv.at[t],
            device_id={"ep": ep, "tp": 1 - tp},
            device_id_type=MESH,
        )

    def finish(t):
        for j in range(t * more * pair, (t + 1) * more * pair):
            scale = scales_ref[j]
            gate = (part_out[j, :, pl.ds(0, ff)] + part_in[j, :, pl.ds(0, ff)]) * scale[0:1]
            up = (part_out[j, :, pl.ds(ff, ff)] + part_in[j, :, pl.ds(ff, ff)]) * scale[1:2]
            units[j] = (gate / (1.0 + jnp.exp(-gate)) * up).astype(jnp.bfloat16)

    def project(k, s, slot):
        begin, deep, count = plan[k]
        for p in range(count):
            j = s * count + p
            total = jnp.dot(
                lines[j, :, pl.ds(begin, deep)],
                unit_buf[slot, pl.ds(p * deep, deep)],
                preferred_element_type=jnp.float32,
            )
            if k > 0:
                total = total + part_out[j]
            part_out[j] = total

    def unit_wait(k, slot):
        _, deep, count = plan[k]
        landed(unit_buf.at[slot, pl.ds(0, deep * count)], unit_sem.at[slot])

    def step(k, s, i, count):
        slots_of = [(i + m) % unit_ring for m in range(count)]
        for slot in slots_of:
            unit_wait(k, slot)
        ends = k == len(plan) - 1
        turn = s // more
        if ends and turn >= lag:
            part_copy(turn - lag).wait_recv()
            finish(turn - lag)
        for m, slot in enumerate(slots_of):
            project(k, s + m, slot)
        if ends:
            part_copy(turn).start()
        for m in range(count):
            if ends:
                start_downs(s + m)
            if i + m < again:
                start_unit(i + m + unit_ring)

    drain(route_in, n_ep - 1, plain_sem.at[0])
    done = 0
    for k in range(len(plan)):
        begin, deep, count = plan[k]
        landed(row_in.at[pl.ds(0, peers - 1), :, part_of(k)], row_recv.at[k])
        select(k)
        total = held // count
        count = more if total % more == 0 else 1
        for s in range(0, total, count):
            step(k, s, done + s, count)
        done += total

    def down(span, c, before):
        for i in span:
            _, wide, count, _ = items[i]
            slot = i % down_ring
            landed(down_buf.at[slot, :, pl.ds(0, count * wide)], down_sem.at[slot])
        for act in before:
            act()
        for i in span:
            _, wide, count, q = items[i]
            slim = wide // fold
            for p in range(count):
                j = q * count + p
                value = jnp.dot(
                    units[j],
                    down_buf[i % down_ring, :, p * wide : (p + 1) * wide],
                    preferred_element_type=jnp.float32,
                ).astype(jnp.bfloat16)
                for f in range(fold):
                    values[c % 2, f, j * slots : (j + 1) * slots, :slim] = value[
                        :, f * slim : (f + 1) * slim
                    ]
        for i in span:
            if i + down_ring < len(items):
                start_down(i + down_ring)

    def window(c):
        return pl.ds(chunks[c][0] // fold, chunks[c][1] // fold)

    def mix(c):
        slim = chunks[c][1] // fold
        mixed = jnp.dot(mixing[0], values[c % 2, 0, :, :slim], preferred_element_type=jnp.float32)
        for f in range(1, fold):
            mixed = mixed + jnp.dot(
                mixing[f], values[c % 2, f, :, :slim], preferred_element_type=jnp.float32
            )
        back_out[:, :, window(c)] = mixed.astype(jnp.bfloat16).reshape(peers, SUBLANES, slim)

    def give(c):
        def act(where, peer, h):
            pltpu.make_async_remote_copy(
                src_ref=back_out.at[peer, :, window(c)],
                dst_ref=back_in.at[me, :, window(c)],
                send_sem=plain_sem.at[3],
                recv_sem=back_recv.at[c],
                device_id=where,
                device_id_type=MESH,
            ).start()

        each_peer(act)
        back_in[me, :, window(c)] = back_out[me, :, window(c)]

    turns = pairs // more

    def last_units():
        for t in range(turns - lag, turns):
            finish(t)

    ready = (turns - lag) * more * pair // chunks[0][2]
    at = 0
    for c in range(len(chunks)):
        count = held // chunks[c][2]
        span = 2 if 0 < c < len(chunks) - 1 and count % 2 == 0 else 1
        for q in range(0, count, span):
            before = []
            if c == 0 and q == ready:
                for t in range(turns - lag, turns):
                    part_copy(t).wait_recv()
                before.append(last_units)
            if c > 0 and q == 0:
                before.append(functools.partial(mix, c - 1))
            down(range(at + q, at + q + span), c, before)
            if c > 0 and q == 0:
                give(c - 1)
        at += count
    mix(len(chunks) - 1)
    give(len(chunks) - 1)

    for c in range(len(chunks)):
        begin, wide, _ = chunks[c]
        slim = wide // fold
        landed(back_in.at[pl.ds(0, peers - 1), :, window(c)], back_recv.at[c])
        for h in range(n_tp):
            total = back_in[h, :, window(c)].astype(jnp.float32)
            for e in range(1, n_ep):
                total = total + back_in[e * n_tp + h, :, window(c)].astype(jnp.float32)
            for f in range(fold):
                at = h * half + begin + f * slim
                out_ref[:, at : at + slim] = total[f * rows : (f + 1) * rows].astype(jnp.bfloat16)
    landed(part_out, plain_sem.at[0])
    drain(row_in, peers - 1, plain_sem.at[2])
    drain(back_in, peers - 1, plain_sem.at[3])


def body(
    hidden,
    norm_gain,
    rot_left,
    rot_right,
    expert_ids,
    gate_weights,
    w_gate,
    w_up,
    w_down,
    unit_scales,
):
    n_ep, n_tp = lax.axis_size("ep"), lax.axis_size("tp")
    peers = n_ep * n_tp
    rows, width = hidden.shape
    group_rows, choices = expert_ids.shape
    held, half, ff = w_gate.shape
    experts = held * n_ep // 2
    capacity = 5 * group_rows * choices // (2 * experts)
    slots = capacity * n_ep
    plan, pieces = passes_of(held, half)
    unit_ring = min(UNIT_RING, len(pieces))
    pairs = held // plan[-1][2]
    turns = pairs // MORE if pairs % MORE == 0 else pairs
    tallest = max(deep * count for _, deep, count in plan)
    chunks, items = chunks_of(held, half)
    down_ring = min(DOWN_RING, len(items))
    broad = max(wide * count for _, wide, count in chunks)
    widest = max(wide for _, wide, _ in chunks)
    fold = SUBLANES // rows
    padded = peers * SUBLANES
    small = (
        hidden,
        norm_gain.reshape(1, width),
        rot_left,
        rot_right,
        expert_ids,
        gate_weights,
        unit_scales,
    )
    return pl.pallas_call(
        functools.partial(kernel, (n_ep, n_tp, capacity)),
        out_shape=pltpu.VMEM((rows, width), jnp.bfloat16),
        in_specs=[pl.BlockSpec(memory_space=pltpu.HBM)] * 10,
        out_specs=pl.BlockSpec(memory_space=pltpu.VMEM),
        scratch_shapes=[pltpu.VMEM(x.shape, x.dtype) for x in small]
        + [
            pltpu.VMEM((unit_ring, tallest, 2 * ff), jnp.bfloat16),
            pltpu.VMEM((down_ring, ff, broad), jnp.bfloat16),
            pltpu.VMEM((n_tp, SUBLANES, half // fold), jnp.bfloat16),
            pltpu.VMEM((peers, SUBLANES, half // fold), jnp.bfloat16),
            pltpu.VMEM((group_rows, capacity * experts), jnp.bfloat16),
            pltpu.VMEM((n_ep, group_rows, capacity * experts), jnp.bfloat16),
            pltpu.VMEM((capacity * experts, padded), jnp.float32),
            pltpu.VMEM((held, slots, half), jnp.bfloat16),
            pltpu.VMEM((held, slots, 2 * ff), jnp.float32),
            pltpu.VMEM((held, slots, 2 * ff), jnp.float32),
            pltpu.VMEM((held, slots, ff), jnp.bfloat16),
            pltpu.VMEM((fold, padded, held * slots), jnp.bfloat16),
            pltpu.VMEM((2, fold, held * slots, widest // fold), jnp.bfloat16),
            pltpu.VMEM((peers, SUBLANES, half // fold), jnp.bfloat16),
            pltpu.VMEM((peers, SUBLANES, half // fold), jnp.bfloat16),
            pltpu.SemaphoreType.DMA((unit_ring,)),
            pltpu.SemaphoreType.DMA((down_ring,)),
            pltpu.SemaphoreType.DMA((turns,)),
            pltpu.SemaphoreType.DMA((len(plan),)),
            pltpu.SemaphoreType.DMA((len(chunks),)),
            pltpu.SemaphoreType.DMA((5,)),
        ],
        compiler_params=pltpu.CompilerParams(
            collective_id=0, has_side_effects=True, vmem_limit_bytes=63 * 1024 * 1024
        ),
    )(*small, w_gate, w_up, w_down)


def solution(mesh):
    placed = (
        P(("groups", "ep", "tp"), None),
        P(),
        P(),
        P(),
        P(("groups", "ep"), None),
        P(("groups", "ep"), None),
        P("ep", "tp", None),
        P("ep", "tp", None),
        P("ep", None, "tp"),
        P("ep", None, None),
    )
    return jax.shard_map(
        body, mesh=mesh, in_specs=placed, out_specs=P(("groups", "ep", "tp"), None), check_vma=False
    )
```

time: 35.2 us -> 32.5 us (0.923)
  Pallas kernels: 34.4 us -> 31.7 us
    pallas_call x1, Pallas kernels: 34.4 us -> 31.7 us  [body(): pl.pallas_call(functools.partial(kernel, (n_ep, n_tp, capacity)), out_sha...]
where the time goes in v2:
time: 32.5 us; the launch traced here: 32.3 us
  Pallas kernels  31.7 us (98%)
  local copies, waits for them, and re-layouts  0.62 us (2%)
    pallas_call x1, Pallas kernels, body(): pl.pallas_call(functools.partial(kernel, (n_ep, n_tp, capacity)), out_sha...  31.7 us

profile of v2, /device:TPU:0, one launch (start us, length us, event | category | flops | bytes accessed | tf_op | source)
XLA Modules:
  0.0 32.3 jit_solution(3853469893649447887)
XLA Ops:
  0.0 31.7 %shard_map.100 = bf16[4,4096]{1,0:T(4,128)(2,1)S(1)} custom-call(bf16[4,4096]{1,0:T(4,128)(2,1)} %hid_hbm.1, f32[1,4096]{1,0:T(1,128)} %bitcast.1, f32[64,64]{1,0:T(8,128)} %left_hbm.1, f32[64,64]{1,0:T(8,128)} %right_hbm.1, s32[8,8]{1,0:T(8,128)} %ids_hbm.1, f32[8,8]{1,0:T(8,128)} %weights_hbm.1, f32[16,2,384]{2,1,0:T(2,128)} %scales_hbm.1, ...), custom_call_target="tpu_custom_call" | custom-call | tf_op jit(solution)/shard_map/pallas_call | solution.py:562
  31.7 0.6 %copy.12 = bf16[4,4096]{1,0:T(4,128)(2,1)} copy(bf16[4,4096]{1,0:T(4,128)(2,1)S(1)} %shard_map.100) | data formatting | bytes 65536

commit v3 on v2

--- a/solution.py
+++ b/solution.py
@@ -14,11 +14,13 @@
 PASSES = (4, 4, 2)
 LAG = 2
 MORE = 2
+SINGLE = 2
+LATE = 4
 SPAN = 5
 UNIT_RING = 14
 DOWN_RING = 9
 EARLY = 3
-WIDTHS = ((1, 8), (2, 4), (2, 4), (2, 4), (1, 4))
+WIDTHS = ((2, 4), (2, 4), (2, 4), (1, 8), (1, 4))
 UNROLL = 32
 
 
@@ -114,6 +116,19 @@
         pieces += [(begin, deep, count, s) for s in range(held // count)]
         begin += deep
     return plan, pieces
+
+
+def blocks_of(count, step):
+    return [(at, min(step, count - at)) for at in range(0, count, step)]
+
+
+def spans_of(count, last):
+    return blocks_of(count - 2, 2) + [(count - 2, 1), (count - 1, 1)] if last and count > 2 else blocks_of(count, 1)
+
+
+def turns_of(pairs):
+    single = min(SINGLE, pairs)
+    return blocks_of(pairs - single, MORE) + [(s, 1) for s in range(pairs - single, pairs)]
 
 
 def chunks_of(held, half):
@@ -163,7 +178,6 @@
     back_out,
     back_in,
     unit_sem,
-    down_sem,
     part_recv,
     row_recv,
     back_recv,
@@ -187,9 +201,10 @@
     plan, pieces = passes_of(held, half)
     pair = plan[-1][2]
     pairs = held // pair
-    more = MORE if pairs % MORE == 0 else 1
-    lag = min(LAG, pairs // more)
+    turns = turns_of(pairs)
+    lag = min(LAG, len(turns))
     again = len(pieces) - unit_ring
+    spare = max(again, 0)
 
     barrier = pltpu.get_barrier_semaphore()
 
@@ -211,7 +226,7 @@
             pltpu.make_async_copy(
                 down_hbm.at[q * count + p, :, pl.ds(begin, wide)],
                 down_buf.at[slot, :, pl.ds(p * wide, wide)],
-                down_sem.at[slot],
+                unit_sem.at[spare + slot],
             ).start()
 
     ahead = -(-down_ring // min(pairs, SPAN))
@@ -361,7 +376,7 @@
             ].reshape(held, slots, thin)
 
     def part_copy(t):
-        span = pl.ds(t * more * pair, more * pair)
+        span = pl.ds(turns[t][0] * pair, turns[t][1] * pair)
         return pltpu.make_async_remote_copy(
             src_ref=part_out.at[span],
             dst_ref=part_in.at[span],
@@ -372,7 +387,7 @@
         )
 
     def finish(t):
-        for j in range(t * more * pair, (t + 1) * more * pair):
+        for j in range(turns[t][0] * pair, (turns[t][0] + turns[t][1]) * pair):
             scale = scales_ref[j]
             gate = (part_out[j, :, pl.ds(0, ff)] + part_in[j, :, pl.ds(0, ff)]) * scale[0:1]
             up = (part_out[j, :, pl.ds(ff, ff)] + part_in[j, :, pl.ds(ff, ff)]) * scale[1:2]
@@ -395,24 +410,22 @@
         _, deep, count = plan[k]
         landed(unit_buf.at[slot, pl.ds(0, deep * count)], unit_sem.at[slot])
 
-    def step(k, s, i, count):
+    def step(k, s, i, count, turn):
         slots_of = [(i + m) % unit_ring for m in range(count)]
         for slot in slots_of:
             unit_wait(k, slot)
-        ends = k == len(plan) - 1
-        turn = s // more
-        if ends and turn >= lag:
+        if turn is not None and turn >= lag:
             part_copy(turn - lag).wait_recv()
             finish(turn - lag)
         for m, slot in enumerate(slots_of):
             project(k, s + m, slot)
-        if ends:
-            part_copy(turn).start()
         for m in range(count):
-            if ends:
-                start_downs(s + m)
             if i + m < again:
                 start_unit(i + m + unit_ring)
+        if turn is not None:
+            part_copy(turn).start()
+            for m in range(count):
+                start_downs(s + m)
 
     drain(route_in, n_ep - 1, plain_sem.at[0])
     done = 0
@@ -421,16 +434,19 @@
         landed(row_in.at[pl.ds(0, peers - 1), :, part_of(k)], row_recv.at[k])
         select(k)
         total = held // count
-        count = more if total % more == 0 else 1
-        for s in range(0, total, count):
-            step(k, s, done + s, count)
+        if k == len(plan) - 1:
+            for t, (at, span) in enumerate(turns):
+                step(k, at, done + at, span, t)
+        else:
+            for at, span in blocks_of(total, MORE):
+                step(k, at, done + at, span, None)
         done += total
 
     def down(span, c, before):
         for i in span:
             _, wide, count, _ = items[i]
             slot = i % down_ring
-            landed(down_buf.at[slot, :, pl.ds(0, count * wide)], down_sem.at[slot])
+            landed(down_buf.at[slot, :, pl.ds(0, count * wide)], unit_sem.at[spare + slot])
         for act in before:
             act()
         for i in span:
@@ -477,28 +493,32 @@
         each_peer(act)
         back_in[me, :, window(c)] = back_out[me, :, window(c)]
 
-    turns = pairs // more
-
-    def last_units():
-        for t in range(turns - lag, turns):
-            finish(t)
-
-    ready = (turns - lag) * more * pair // chunks[0][2]
+    finished = len(turns) - lag
+
+    def meet(experts):
+        nonlocal finished
+        acts = []
+        while finished < len(turns) and turns[finished][0] * pair < experts:
+            part_copy(finished).wait_recv()
+            acts.append(functools.partial(finish, finished))
+            finished += 1
+        return acts
+
     at = 0
     for c in range(len(chunks)):
-        count = held // chunks[c][2]
-        span = 2 if 0 < c < len(chunks) - 1 and count % 2 == 0 else 1
-        for q in range(0, count, span):
-            before = []
-            if c == 0 and q == ready:
-                for t in range(turns - lag, turns):
-                    part_copy(t).wait_recv()
-                before.append(last_units)
-            if c > 0 and q == 0:
+        _, _, each_item = chunks[c]
+        count = held // each_item
+        late = c >= len(chunks) - LATE
+        for q, span in spans_of(count, c == len(chunks) - 1):
+            before = meet((q + span) * each_item)
+            if late and q == 0:
                 before.append(functools.partial(mix, c - 1))
             down(range(at + q, at + q + span), c, before)
-            if c > 0 and q == 0:
+            if late and q == 0:
                 give(c - 1)
+        if c < len(chunks) - 1 - LATE:
+            mix(c)
+            give(c)
         at += count
     mix(len(chunks) - 1)
     give(len(chunks) - 1)
@@ -542,7 +562,7 @@
     plan, pieces = passes_of(held, half)
     unit_ring = min(UNIT_RING, len(pieces))
     pairs = held // plan[-1][2]
-    turns = pairs // MORE if pairs % MORE == 0 else pairs
+    turns = len(turns_of(pairs))
     tallest = max(deep * count for _, deep, count in plan)
     chunks, items = chunks_of(held, half)
     down_ring = min(DOWN_RING, len(items))
@@ -581,8 +601,7 @@
             pltpu.VMEM((2, fold, held * slots, widest // fold), jnp.bfloat16),
             pltpu.VMEM((peers, SUBLANES, half // fold), jnp.bfloat16),
             pltpu.VMEM((peers, SUBLANES, half // fold), jnp.bfloat16),
-            pltpu.SemaphoreType.DMA((unit_ring,)),
-            pltpu.SemaphoreType.DMA((down_ring,)),
+            pltpu.SemaphoreType.DMA((max(unit_ring, len(pieces) - unit_ring + down_ring),)),
             pltpu.SemaphoreType.DMA((turns,)),
             pltpu.SemaphoreType.DMA((len(plan),)),
             pltpu.SemaphoreType.DMA((len(chunks),)),

time: 32.5 us -> 32.2 us (level)
  no operation moved by 1% of the time
where the time goes in v3:
time: 32.2 us; the launch traced here: 32.1 us
  Pallas kernels  31.4 us (98%)
  local copies, waits for them, and re-layouts  0.62 us (2%)
    pallas_call x1, Pallas kernels, body(): pl.pallas_call(functools.partial(kernel, (n_ep, n_tp, capacity)), out_sha...  31.4 us

profile of v3, /device:TPU:0, one launch (start us, length us, event | category | flops | bytes accessed | tf_op | source)
XLA Modules:
  0.0 32.1 jit_solution(822097876880175819)
XLA Ops:
  0.0 31.4 %shard_map.100 = bf16[4,4096]{1,0:T(4,128)(2,1)S(1)} custom-call(bf16[4,4096]{1,0:T(4,128)(2,1)} %hid_hbm.1, f32[1,4096]{1,0:T(1,128)} %bitcast.1, f32[64,64]{1,0:T(8,128)} %left_hbm.1, f32[64,64]{1,0:T(8,128)} %right_hbm.1, s32[8,8]{1,0:T(8,128)} %ids_hbm.1, f32[8,8]{1,0:T(8,128)} %weights_hbm.1, f32[16,2,384]{2,1,0:T(2,128)} %scales_hbm.1, ...), custom_call_target="tpu_custom_call" | custom-call | tf_op jit(solution)/shard_map/pallas_call | solution.py:582
  31.4 0.6 %copy.12 = bf16[4,4096]{1,0:T(4,128)(2,1)} copy(bf16[4,4096]{1,0:T(4,128)(2,1)S(1)} %shard_map.100) | data formatting | bytes 65536

commit v4 on v3

--- a/solution.py
+++ b/solution.py
@@ -20,7 +20,7 @@
 UNIT_RING = 14
 DOWN_RING = 9
 EARLY = 3
-WIDTHS = ((2, 4), (2, 4), (2, 4), (1, 8), (1, 4))
+WIDTHS = ((2, 4), (2, 4), (2, 4), (1, 8), (1, 8))
 UNROLL = 32
 
 
@@ -279,19 +279,21 @@
             (right_hbm, right_ref),
             (ids_hbm, ids_ref),
             (weights_hbm, weights_ref),
-            (scales_hbm, scales_ref),
         )
     ]
+    scales_copy = pltpu.make_async_copy(scales_hbm, scales_ref, plain_sem.at[5])
     for copy in small:
         copy.start()
+    start_unit(0)
     each_peer(
         lambda where, peer, h: pl.semaphore_signal(
             barrier, inc=1, device_id=where, device_id_type=MESH
         )
     )
     early = min(EARLY, unit_ring)
-    for i in range(early):
+    for i in range(1, early):
         start_unit(i)
+    scales_copy.start()
     for copy in small:
         copy.wait()
 
@@ -428,6 +430,7 @@
                 start_downs(s + m)
 
     drain(route_in, n_ep - 1, plain_sem.at[0])
+    scales_copy.wait()
     done = 0
     for k in range(len(plan)):
         begin, deep, count = plan[k]
@@ -605,7 +608,7 @@
             pltpu.SemaphoreType.DMA((turns,)),
             pltpu.SemaphoreType.DMA((len(plan),)),
             pltpu.SemaphoreType.DMA((len(chunks),)),
-            pltpu.SemaphoreType.DMA((5,)),
+            pltpu.SemaphoreType.DMA((6,)),
         ],
         compiler_params=pltpu.CompilerParams(
             collective_id=0, has_side_effects=True, vmem_limit_bytes=63 * 1024 * 1024

time: 32.2 us -> 32.1 us (level)
  no operation moved by 1% of the time
where the time goes in v4:
time: 32.1 us; the launch traced here: 32 us
  Pallas kernels  31.4 us (98%)
  local copies, waits for them, and re-layouts  0.62 us (2%)
    pallas_call x1, Pallas kernels, body(): pl.pallas_call(functools.partial(kernel, (n_ep, n_tp, capacity)), out_sha...  31.4 us

profile of v4, /device:TPU:0, one launch (start us, length us, event | category | flops | bytes accessed | tf_op | source)
XLA Modules:
  0.0 32.0 jit_solution(14968484378281817509)
XLA Ops:
  0.0 31.4 %shard_map.100 = bf16[4,4096]{1,0:T(4,128)(2,1)S(1)} custom-call(bf16[4,4096]{1,0:T(4,128)(2,1)} %hid_hbm.1, f32[1,4096]{1,0:T(1,128)} %bitcast.1, f32[64,64]{1,0:T(8,128)} %left_hbm.1, f32[64,64]{1,0:T(8,128)} %right_hbm.1, s32[8,8]{1,0:T(8,128)} %ids_hbm.1, f32[8,8]{1,0:T(8,128)} %weights_hbm.1, f32[16,2,384]{2,1,0:T(2,128)} %scales_hbm.1, ...), custom_call_target="tpu_custom_call" | custom-call | tf_op jit(solution)/shard_map/pallas_call | solution.py:585
  31.4 0.6 %copy.12 = bf16[4,4096]{1,0:T(4,128)(2,1)} copy(bf16[4,4096]{1,0:T(4,128)(2,1)S(1)} %shard_map.100) | data formatting | bytes 65536
